TPU v7x, 32 devices: a whole 2x2x4 slice. The times are simulated.
32 devices in a mesh: alt: 2 (over x), strip: 16 (over z, y, core).
Axes of the slice: x: 2, y: 2, z: 4, core: 2. Of those that a mesh axis runs over, the one named last changes fastest.
Arguments:
- screens: bfloat16 [4, 512, 512], P('alt', 'strip'), may hold values from -2.390625 to 2.390625
- row_offset: int32 [2, 4, 2], replicated, may hold values from 0 to 341, as said below
- col_offset: int32 [2, 4, 2], replicated, may hold values from 0 to 341, as said below
- layer_bin: int32 [4], replicated, may hold values from 0 to 15
- illumination: float32 [16, 12800], P(None, ('alt', 'strip')), may hold values from 0.3 to 1
- reconstructor: bfloat16 [2, 12800, 6000], P(None, ('alt', 'strip')), may hold values from -0.0390625 to 0.0390625
- sat_code: int32 [6000], replicated, may hold values from 1 to 16
Outputs:
- slopes: float32 [2, 2, 12800], P(None, None, ('alt', 'strip'))
- commands: float32 [2, 6000], replicated
Inputs may be any that keep to these rules, and one draw needn't show every extreme that they name: Every footprint lies inside the screen: row_offset[f, l, g] + (319) shrink_l <= 511. Every footprint lies inside the screen: col_offset[f, l, g] + (319) shrink_l <= 511.
All inputs are finite; a program needn't handle non-finite values.
Results may differ from a plain program's by a relative error of at most 0.0028.
Values sent between devices are 32-bit elements; how exact they have to be, the bound alone decides.
A program may use at most 64 MiB of HBM per device.

v0:
```python
import functools
import math

import jax
import jax.numpy as jnp
from jax import lax
from jax.experimental import pallas as pl
from jax.experimental.pallas import tpu as pltpu
from jax.sharding import PartitionSpec as P

LENSLETS = 80
PIXELS = 4
GUIDE_STARS = 2
FRAMES = 2
ACTUATORS = 6000
PUPIL_PIX = 320
WINDOW = 384
SUBAPS_ALL = 12800


highest = lax.Precision.HIGHEST
loop_gain = 0.5
code_step = 0.125
bin_step = 0.03125


def bilinear(offsets):
    return jnp.maximum(0.0, 1.0 - jnp.abs(offsets))


def dft_tables():
    padded = 2 * PIXELS
    freq_index = jnp.arange(padded * padded, dtype=jnp.int32)
    freq_row = freq_index // padded
    freq_col = freq_index % padded
    pix_index = jnp.arange(PIXELS * PIXELS, dtype=jnp.int32)
    pix_row = pix_index // PIXELS
    pix_col = pix_index % PIXELS
    turn_count = (
        freq_row[:, None] * pix_row[None, :] + freq_col[:, None] * pix_col[None, :]
    ) % padded
    angles = turn_count.astype(jnp.float32) * (2.0 * math.pi / padded)
    coord_row = ((freq_row + PIXELS) % padded - PIXELS).astype(jnp.float32)
    coord_col = ((freq_col + PIXELS) % padded - PIXELS).astype(jnp.float32)
    return (jnp.cos(angles), jnp.sin(angles), coord_row, coord_col)


def centroids(pupil_phase, illumination, tables):
    cosine, sine_table, coord_row, coord_col = tables
    field_re = illumination * jnp.cos(pupil_phase)
    field_im = illumination * jnp.sin(pupil_phase)
    real_part = jnp.dot(cosine, field_re, precision=highest) + jnp.dot(
        sine_table, field_im, precision=highest
    )
    imag_part = jnp.dot(cosine, field_im, precision=highest) - jnp.dot(
        sine_table, field_re, precision=highest
    )
    intensity = real_part * real_part + imag_part * imag_part
    flux_sum = jnp.sum(intensity, axis=0)
    slope_row = jnp.sum(intensity * coord_row[:, None], axis=0) / flux_sum
    slope_col = jnp.sum(intensity * coord_col[:, None], axis=0) / flux_sum
    return jnp.stack([slope_row, slope_col])


def shards(screens, row_offset, col_offset, layer_bin, illumination, reconstructor, sat_code):
    layer_dev = screens.shape[0]
    rows_here = screens.shape[1]
    count_here = illumination.shape[1]
    group_pos = lax.axis_index("alt")
    strip_pos = lax.axis_index("strip")
    row_global = strip_pos * rows_here + jnp.arange(rows_here, dtype=jnp.int32)
    pupil_idx = jnp.arange(PUPIL_PIX, dtype=jnp.float32)
    window_idx = jnp.arange(WINDOW, dtype=jnp.float32)
    widened_layers = [
        jnp.pad(screens[layer_no], ((0, 0), (0, WINDOW))) for layer_no in range(layer_dev)
    ]
    frame_terms = []
    for frame_no in range(FRAMES):
        running = jnp.zeros((PIXELS, PIXELS, GUIDE_STARS, LENSLETS, LENSLETS), jnp.float32)
        for layer_no in range(layer_dev):
            layer_pos = group_pos * layer_dev + layer_no
            tops = lax.dynamic_index_in_dim(row_offset[frame_no], layer_pos, 0, keepdims=False)
            lefts = lax.dynamic_index_in_dim(col_offset[frame_no], layer_pos, 0, keepdims=False)
            bin_value = lax.dynamic_index_in_dim(layer_bin, layer_pos, 0, keepdims=False)
            shrink = 1.0 - bin_value.astype(jnp.float32) * bin_step
            col_weights = bilinear(window_idx[None, :] - pupil_idx[:, None] * shrink)
            widened = widened_layers[layer_no]

            def cut_columns(left_col):
                return lax.dynamic_slice_in_dim(widened, left_col, WINDOW, 1)

            strips = jax.vmap(cut_columns)(lefts).astype(jnp.float32)
            across = jnp.einsum("drc,jc->drj", strips, col_weights, precision=highest)
            offsets = (row_global[None, :] - tops[:, None]).astype(jnp.float32)
            row_weights = bilinear(offsets[:, None, :] - pupil_idx[None, :, None] * shrink)
            running = running + jnp.einsum(
                "dapr,drbq->pqdab",
                row_weights.reshape(GUIDE_STARS, LENSLETS, PIXELS, rows_here),
                across.reshape(GUIDE_STARS, rows_here, LENSLETS, PIXELS),
                precision=highest,
            )
        frame_terms.append(running.reshape(PIXELS * PIXELS, SUBAPS_ALL))
    phase_terms = jnp.concatenate(frame_terms, axis=0)
    partly = lax.psum_scatter(phase_terms, "alt", scatter_dimension=1, tiled=True)
    owned = lax.psum_scatter(partly, "strip", scatter_dimension=1, tiled=True)
    pupil_phase = owned.reshape(FRAMES, PIXELS * PIXELS, count_here)
    tables = dft_tables()
    slopes = jnp.stack(
        [centroids(pupil_phase[frame_no], illumination, tables) for frame_no in range(FRAMES)]
    )
    rounded = slopes.astype(jnp.bfloat16).reshape(FRAMES, 2 * count_here)
    partial_value = jnp.dot(
        rounded,
        reconstructor.reshape(2 * count_here, ACTUATORS),
        preferred_element_type=jnp.float32,
    )
    updates = lax.psum(partial_value, ("alt", "strip"))
    limits = sat_code.astype(jnp.float32) * code_step
    first_cmd = jnp.clip(loop_gain * updates[0], -limits, limits)
    second_cmd = jnp.clip(first_cmd + loop_gain * updates[1], -limits, limits)
    return (slopes, jnp.stack([first_cmd, second_cmd]))


MESH = pl.DeviceIdType.MESH


def pair_gain(distance):
    turn = 2.0 * math.pi / (2 * PIXELS)
    return 4.0 * sum(k * math.sin(turn * k * distance) for k in range(1, PIXELS))


SPLIT = 2


def padded_rows(arcs):
    return -(-arcs * FRAMES * PIXELS // 16) * 16


def packed_rows(arcs):
    full = PUPIL_PIX // 128
    return FRAMES * PIXELS * (full * arcs + (arcs + 1) // 2)


def fused_kernel(
    depth,
    block,
    scr_hbm,
    row_hbm,
    col_hbm,
    bin_hbm,
    ill_hbm,
    rec_hbm,
    slopes_out,
    upd_out,
    scr_ref,
    row_ref,
    col_ref,
    bin_ref,
    ill_ref,
    scr_all,
    colw,
    roww,
    rhs,
    acc,
    ysend,
    yown,
    yrecv,
    zsend,
    zrecv,
    phiq,
    illq,
    slope_sc,
    rec,
    upd,
    part,
    zsum,
    fin,
    in_sem,
    rec_sem,
    x_send,
    x_recv,
    core_send,
    core_recv,
    fwd_send,
    fwd_recv,
    y_send,
    y_recv,
    z_send,
    z_recv,
    a_send,
    a_recv,
    b_send,
    b_recv,
    c_send,
    c_recv,
):
    layer_dev, rows_here, columns = scr_ref.shape
    count_here = ill_ref.shape[1]
    arcs = count_here // LENSLETS
    chunk_rows = padded_rows(arcs)
    full = PUPIL_PIX // 128
    rest = PUPIL_PIX - full * 128
    rows_chip = 2 * rows_here
    actuators = rec_hbm.shape[2]

    loads = [
        pltpu.make_async_copy(src, dst, in_sem.at[n])
        for n, (src, dst) in enumerate(
            (
                (scr_hbm, scr_ref),
                (row_hbm, row_ref),
                (col_hbm, col_ref),
                (bin_hbm, bin_ref),
                (ill_hbm, ill_ref),
            )
        )
    ]
    for load in loads:
        load.start()
    rec_copy = pltpu.make_async_copy(rec_hbm, rec, rec_sem)
    rec_copy.start()

    x = lax.axis_index("alt")
    strip = lax.axis_index("strip")
    core = strip % 2
    y = (strip // 2) % 2
    z = strip // 4
    me = (x * 2 + y) * 2 + core

    offsets = ((1, 1, 0), (1, 1, 1), (1, 0, 0), (1, 0, 1), (0, 1, 0), (0, 1, 1), (0, 0, 1))

    def place(n):
        dx, dy, dc = offsets[n]
        return ((x + dx) % 2, (y + dy) % 2, (core + dc) % 2)

    def plane(n):
        px, py, pc = place(n)
        return (px, (z * 2 + py) * 2 + pc)

    def slot(n):
        px, py, pc = place(n)
        return (px * 2 + py) * 2 + pc

    def depth_dev(zpos):
        return (x, (zpos * 2 + y) * 2 + core)

    barrier = pltpu.get_barrier_semaphore()
    for n in range(7):
        pl.semaphore_signal(barrier, inc=1, device_id=plane(n), device_id_type=MESH)
    for k in range(1, depth):
        pl.semaphore_signal(barrier, inc=1, device_id=depth_dev((z + k) % depth), device_id_type=MESH)

    own = pl.ds(x * layer_dev, layer_dev)
    loads[0].wait()
    for li in range(layer_dev):
        scr_all[core, x * layer_dev + li] = scr_ref[li].astype(jnp.float32)
    pl.semaphore_wait(barrier, 7 + depth - 1)

    def remote(src, dst, send, recv, device):
        copy = pltpu.make_async_remote_copy(
            src_ref=src, dst_ref=dst, send_sem=send, recv_sem=recv, device_id=device, device_id_type=MESH
        )
        copy.start()
        return copy

    own_block = scr_all.at[core, own]
    x_copies = []
    for li in range(layer_dev):
        piece = scr_all.at[core, x * layer_dev + li]
        x_copies.append(remote(piece, piece, x_send.at[li], x_recv.at[li], (1 - x, strip)))
    core_dev = (x, (z * 2 + y) * 2 + 1 - core)
    core_copy = remote(own_block, own_block, core_send, core_recv, core_dev)

    for load in loads[1:]:
        load.wait()
    col_pos = lax.broadcasted_iota(jnp.int32, (columns, PUPIL_PIX), 0).astype(jnp.float32)
    lane = lax.broadcasted_iota(jnp.int32, (1, PUPIL_PIX), 1)
    q_of = (
        (lane >= LENSLETS).astype(jnp.int32)
        + (lane >= 2 * LENSLETS).astype(jnp.int32)
        + (lane >= 3 * LENSLETS).astype(jnp.int32)
    )
    pupil_col = ((lane - q_of * LENSLETS) * PIXELS + q_of).astype(jnp.float32)
    row_lane = lax.broadcasted_iota(jnp.int32, (chunk_rows, 2 * rows_chip), 1)
    row_pos = (row_lane % rows_chip + (z * 2 + y) * rows_chip).astype(jnp.float32)
    row_sub = lax.broadcasted_iota(jnp.int32, (chunk_rows, 2 * rows_chip), 0)
    row_base = (row_sub // 8) * PIXELS + row_sub % PIXELS
    row_frame = (row_sub // PIXELS) % FRAMES
    seg = 2 * rows_chip
    groups = [(rel, li) for rel in range(2) for li in range(layer_dev)]

    for rel, li in groups:
        layer = ((x + rel) % 2) * layer_dev + li
        shrink = 1.0 - bin_ref[layer].astype(jnp.float32) * bin_step
        reach = pupil_col * shrink
        for f in range(FRAMES):
            left = col_ref[f, x, layer].astype(jnp.float32)
            weight = bilinear(col_pos - (reach + left))
            colw[f, rel * layer_dev + li] = weight.astype(jnp.bfloat16)

    tops = [
        [row_ref[f, x, ((x + rel) % 2) * layer_dev + li].astype(jnp.float32) for rel, li in groups]
        for f in range(FRAMES)
    ]
    shrinks = [
        1.0 - bin_ref[((x + rel) % 2) * layer_dev + li].astype(jnp.float32) * bin_step for rel, li in groups
    ]
    for zpos in range(depth):
        for ypos in range(2):
            first = ((zpos * 2 + ypos) * 2 + core) * (arcs * PIXELS)
            pupil_row = (row_base + first).astype(jnp.float32)
            for f in range(FRAMES):
                for n in range(len(groups)):
                    weight = bilinear(row_pos - tops[f][n] - pupil_row * shrinks[n])
                    weight = jnp.where(row_frame == f, weight, 0.0)
                    at = (n * FRAMES + f) * seg
                    roww[ypos, zpos * chunk_rows : (zpos + 1) * chunk_rows, at : at + seg] = weight.astype(
                        jnp.bfloat16
                    )
    for p in range(PIXELS):
        for q in range(PIXELS):
            for f in range(FRAMES):
                illq[q, f * PIXELS + p : f * PIXELS + p + 1, :] = ill_ref[p * PIXELS + q : p * PIXELS + q + 1, :]

    def across(rel, layers):
        for li in layers:
            layer = ((x + rel) % 2) * layer_dev + li
            rows = scr_all[:, layer].reshape(rows_chip, columns).astype(jnp.bfloat16)
            for f in range(FRAMES):
                value = jnp.dot(rows, colw[f, rel * layer_dev + li], preferred_element_type=jnp.float32)
                high = value.astype(jnp.bfloat16)
                low = (value - high.astype(jnp.float32)).astype(jnp.bfloat16)
                at = ((rel * layer_dev + li) * FRAMES + f) * seg
                rhs[at : at + rows_chip, :] = high
                rhs[at + rows_chip : at + seg, :] = low

    core_copy.wait()
    def project(ypos, lo, hi):
        value = jnp.dot(roww[ypos, :, lo:hi], rhs[lo:hi, :], preferred_element_type=jnp.float32)
        return value.reshape(depth, chunk_rows, PUPIL_PIX)

    step = FRAMES * seg
    across(0, range(layer_dev))
    fwd_copies = []
    for li in range(layer_dev):
        if li == 1:
            for ypos in range(2):
                acc[ypos] = project(ypos, 0, layer_dev * step)
        x_copies[li].wait_recv()
        piece = scr_all.at[core, (1 - x) * layer_dev + li]
        fwd_copies.append(remote(piece, piece, fwd_send.at[li], fwd_recv.at[li], core_dev))
    for li in range(layer_dev):
        fwd_copies[li].wait()
        across(1, [li])
        if li < layer_dev - 1:
            for ypos in range(2):
                acc[ypos] += project(ypos, (layer_dev + li) * step, (layer_dev + li + 1) * step)
    last = (2 * layer_dev - 1) * step

    def finish(ypos, zpos, out):
        rows = pl.ds(pl.multiple_of(zpos * chunk_rows, chunk_rows), chunk_rows)
        value = jnp.dot(roww[ypos, rows, last:], rhs[last:, :], preferred_element_type=jnp.float32)
        value = value + acc[ypos, zpos]
        for a in range(arcs):
            part_rows = value[a * 8 : (a + 1) * 8]
            for t in range(full):
                at = (t * arcs + a) * 8
                out[zpos, at : at + 8, :] = part_rows[:, t * 128 : (t + 1) * 128]
            at = (full * arcs + a // 2) * 8
            lane0 = (a % 2) * rest
            out[zpos, at : at + 8, lane0 : lane0 + rest] = part_rows[:, full * 128 :]
        if arcs % 2:
            out[zpos, at : at + 8, rest:] = jnp.zeros((8, 128 - rest), jnp.float32)

    for copy in x_copies:
        copy.wait_send()

    order = []
    for n in range(depth - 1):
        down = depth - 1 - n
        down = down - (down <= z).astype(jnp.int32)
        up = n + (n >= z).astype(jnp.int32)
        order.append(jnp.where(2 * z < depth, down, up))
    order.append(z)
    y_dev = (x, (z * 2 + 1 - y) * 2 + core)
    tiles = ysend.shape[1] // 8
    cuts = [8 * (tiles * i // SPLIT) for i in range(SPLIT + 1)]
    pieces = [pl.ds(lo, hi - lo) for lo, hi in zip(cuts[:-1], cuts[1:])]
    y_copies = []
    for n, zpos in enumerate(order):
        finish(1 - y, zpos, ysend)
        for i, rows in enumerate(pieces):
            sem = n * SPLIT + i
            y_copies.append(
                remote(ysend.at[zpos, rows], yrecv.at[n, rows], y_send.at[sem], y_recv.at[sem], y_dev)
            )
    for zpos in order:
        finish(y, zpos, yown)
    z_copies = []
    for n, zpos in enumerate(order):
        for i, rows in enumerate(pieces):
            y_copies[n * SPLIT + i].wait()
            zsend[n, rows] = yown[zpos, rows] + yrecv[n, rows]
            if n < depth - 1:
                z_copies.append(
                    remote(
                        zsend.at[n, rows],
                        zrecv.at[z, rows],
                        z_send.at[n * SPLIT + i],
                        z_recv.at[z * SPLIT + i],
                        depth_dev(zpos),
                    )
                )
    for copy in z_copies:
        copy.wait_send()
    phase = zsend[depth - 1]
    for k in range(1, depth):
        zpos = (z + k) % depth
        for i, rows in enumerate(pieces):
            pltpu.make_async_remote_copy(
                src_ref=zsend.at[0, rows],
                dst_ref=zrecv.at[zpos, rows],
                send_sem=z_send.at[i],
                recv_sem=z_recv.at[zpos * SPLIT + i],
                device_id=depth_dev(zpos),
                device_id_type=MESH,
            ).wait_recv()
        phase = phase + zrecv[zpos]
    zsend[0] = phase
    for a in range(arcs):
        for q in range(PIXELS):
            lo = q * LENSLETS
            while lo < (q + 1) * LENSLETS:
                t = lo // 128
                hi = min((q + 1) * LENSLETS, (t + 1) * 128)
                if t < full:
                    at, lane0 = (t * arcs + a) * 8, lo - t * 128
                else:
                    at, lane0 = (full * arcs + a // 2) * 8, (a % 2) * rest + lo - t * 128
                to = a * LENSLETS + lo - q * LENSLETS
                phiq[q, :, to : to + hi - lo] = zsend[0, at : at + 8, lane0 : lane0 + hi - lo]
                lo = hi

    cosines, sines = [], []
    flux = None
    for q in range(PIXELS):
        amp = illq[q]
        phi = phiq[q]
        cosines.append(amp * jnp.cos(phi))
        sines.append(amp * jnp.sin(phi))
        flux = amp * amp if flux is None else flux + amp * amp
    tip = -float(PIXELS) * flux
    tilt = tip
    pix_row = lax.broadcasted_iota(jnp.int32, flux.shape, 0) % PIXELS
    for d in range(1, PIXELS):
        gain = pair_gain(d)
        even = -2.0 * PIXELS * (-1.0) ** d
        term = None
        for q in range(d, PIXELS):
            ch, sh, cl, sl = cosines[q], sines[q], cosines[q - d], sines[q - d]
            new = gain * (sh * cl - ch * sl) + even * (ch * cl + sh * sl)
            term = new if term is None else term + new
        tilt = tilt + term
        term = None
        for q in range(PIXELS):
            ch, sh = cosines[q], sines[q]
            cl, sl = pltpu.roll(ch, d, 0), pltpu.roll(sh, d, 0)
            new = gain * (sh * cl - ch * sl) + even * (ch * cl + sh * sl)
            term = new if term is None else term + new
        tip = tip + jnp.where(pix_row >= d, term, 0.0)
    for f in range(FRAMES):
        rows = slice(f * PIXELS, (f + 1) * PIXELS)
        total = jnp.sum(flux[rows], axis=0, keepdims=True) * (2.0 * PIXELS)
        for c, value in enumerate((tip, tilt)):
            slope = jnp.sum(value[rows], axis=0, keepdims=True) / total
            slopes_out[f, c : c + 1, :] = slope
            slope_sc[c, f : f + 1, :] = slope

    rec_copy.wait()
    rounded = [slope_sc[c].astype(jnp.bfloat16) for c in range(2)]
    tail = actuators - 6 * block

    def update(chip):
        def some(cols, width):
            value = jnp.dot(rounded[0], rec[0, :, cols], preferred_element_type=jnp.float32)
            value = value + jnp.dot(rounded[1], rec[1, :, cols], preferred_element_type=jnp.float32)
            upd[2 * chip] = value[:, :block]
            upd[2 * chip + 1, :, : width - block] = value[:, block:]

        @pl.when(chip < 3)
        def _():
            some(pl.ds(pl.multiple_of(chip * 2 * block, 128), 2 * block), 2 * block)

        @pl.when(chip == 3)
        def _():
            upd[7] = jnp.zeros_like(upd[7])
            some(slice(6 * block, actuators), tail)

    copies = []
    for n in range(7):
        to = slot(n)
        if n % 2 == 0:
            update(to // 2)
        copies.append(remote(upd.at[to], part.at[n], a_send.at[n], a_recv.at[n], plane(n)))
    for copy in copies:
        copy.wait()
    total = upd[me]
    for n in range(7):
        total = total + part[n]
    zsum[z] = total
    copies = []
    for k in range(1, depth):
        copies.append(
            remote(zsum.at[z], zsum.at[z], b_send.at[k - 1], b_recv.at[k - 1], depth_dev((z + k) % depth))
        )
    for copy in copies:
        copy.wait()
    total = zsum[0]
    for k in range(1, depth):
        total = total + zsum[k]
    fin[me] = total
    copies = []
    for n in range(7):
        copies.append(remote(fin.at[me], fin.at[me], c_send.at[n], c_recv.at[n], plane(n)))
    for copy in copies:
        copy.wait()
    for j in range(8):
        upd_out[:, j * block : (j + 1) * block] = fin[j]


def fused_shards(screens, row_offset, col_offset, layer_bin, illumination, reconstructor, sat_code):
    layer_dev, rows_here, columns = screens.shape
    count_here = illumination.shape[1]
    actuators = reconstructor.shape[2]
    depth = lax.axis_size("strip") // 4
    arcs = count_here // LENSLETS
    chunk = (packed_rows(arcs), 128)
    rows = padded_rows(arcs)
    block = -(-actuators // (8 * 128)) * 128
    contraction = FRAMES * 2 * layer_dev * 2 * 2 * rows_here
    dma = pltpu.SemaphoreType.DMA
    spots = (FRAMES, GUIDE_STARS, row_offset.shape[1])
    vmem = pl.BlockSpec(memory_space=pltpu.VMEM)
    slopes, updates = pl.pallas_call(
        functools.partial(fused_kernel, depth, block),
        out_shape=(
            jax.ShapeDtypeStruct((FRAMES, 2, count_here), jnp.float32),
            jax.ShapeDtypeStruct((FRAMES, 8 * block), jnp.float32),
        ),
        in_specs=[pl.BlockSpec(memory_space=pltpu.HBM)] * 6,
        out_specs=(vmem, vmem),
        scratch_shapes=[
            pltpu.VMEM(screens.shape, jnp.bfloat16),
            pltpu.SMEM(spots, jnp.int32),
            pltpu.SMEM(spots, jnp.int32),
            pltpu.SMEM(layer_bin.shape, jnp.int32),
            pltpu.VMEM(illumination.shape, jnp.float32),
            pltpu.VMEM((2, 2 * layer_dev, rows_here, columns), jnp.float32),
            pltpu.VMEM((FRAMES, 2 * layer_dev, columns, PUPIL_PIX), jnp.bfloat16),
            pltpu.VMEM((2, depth * rows, contraction), jnp.bfloat16),
            pltpu.VMEM((contraction, PUPIL_PIX), jnp.bfloat16),
            pltpu.VMEM((2, depth, rows, PUPIL_PIX), jnp.float32),
            pltpu.VMEM((depth,) + chunk, jnp.float32),
            pltpu.VMEM((depth,) + chunk, jnp.float32),
            pltpu.VMEM((depth,) + chunk, jnp.float32),
            pltpu.VMEM((depth,) + chunk, jnp.float32),
            pltpu.VMEM((depth,) + chunk, jnp.float32),
            pltpu.VMEM((PIXELS, FRAMES * PIXELS, count_here), jnp.float32),
            pltpu.VMEM((PIXELS, FRAMES * PIXELS, count_here), jnp.float32),
            pltpu.VMEM((2, FRAMES, count_here), jnp.float32),
            pltpu.VMEM(reconstructor.shape, jnp.bfloat16),
            pltpu.VMEM((8, FRAMES, block), jnp.float32),
            pltpu.VMEM((7, FRAMES, block), jnp.float32),
            pltpu.VMEM((depth, FRAMES, block), jnp.float32),
            pltpu.VMEM((8, FRAMES, block), jnp.float32),
            dma((5,)), dma, dma((layer_dev,)), dma((layer_dev,)), dma, dma, dma((layer_dev,)), dma((layer_dev,)),
            dma((depth * SPLIT,)), dma((depth * SPLIT,)),
            dma(((depth - 1) * SPLIT,)), dma((depth * SPLIT,)),
            dma((7,)), dma((7,)),
            dma((depth - 1,)), dma((depth - 1,)),
            dma((7,)), dma((7,)),
        ],
        compiler_params=pltpu.CompilerParams(collective_id=0, has_side_effects=True, vmem_limit_bytes=67043328),
        name="fused",
    )(screens, row_offset.transpose(0, 2, 1), col_offset.transpose(0, 2, 1), layer_bin, illumination, reconstructor)
    updates = updates[:, :actuators]
    limits = sat_code.astype(jnp.float32) * code_step
    first_cmd = jnp.clip(loop_gain * updates[0], -limits, limits)
    second_cmd = jnp.clip(first_cmd + loop_gain * updates[1], -limits, limits)
    return (slopes, jnp.stack([first_cmd, second_cmd]))


def solution(mesh):
    alt, strips = mesh.shape["alt"], mesh.shape["strip"]
    fused = alt == 2 == GUIDE_STARS and strips % 4 == 0 and strips > 4 and LENSLETS % strips == 0

    placed = (
        P("alt", "strip", None),
        P(),
        P(),
        P(),
        P(None, ("alt", "strip")),
        P(None, ("alt", "strip"), None),
        P(),
    )
    return jax.shard_map(
        fused_shards if fused else shards,
        mesh=mesh,
        in_specs=placed,
        out_specs=(P(None, None, ("alt", "strip")), P()),
        check_vma=False,
    )
```

profile of v0, /device:TPU:0, one launch (start us, length us, event | category | flops | bytes accessed | tf_op | source)
XLA Modules:
  0.0 36.9 jit_solution(2129843637360555696)
XLA Ops:
  0.6 32.4 %fused.1 = (f32[2,2,400]{2,1,0:T(2,128)}, f32[2,6144]{1,0:T(2,128)}) custom-call(bf16[2,32,512]{2,1,0:T(8,128)(2,1)} %scr_hbm.1, s32[2,2,4]{2,1,0:T(2,128)} %bitcast.2, s32[2,2,4]{2,1,0:T(2,128)} %bitcast.3, s32[4]{0:T(128)} %bin_hbm.1, f32[16,400]{1,0:T(8,128)} %ill_hbm.1, bf16[2,400,6000]{2,1,0:T(8,128)(2,1)} %rec_hbm.1), custom_call_target="tpu_custom_call" | custom-call | tf_op jit(solution)/shard_map/fused/pallas_call | solution.py:544
  33.1 1.0 %multiply_reduce_fusion.1 = (f32[6000]{0:T(1024)S(1)}, f32[6000]{0:T(1024)S(1)}) fusion(f32[2,6144]{1,0:T(2,128)} %get-tuple-element.5), kind=kLoop, calls=%fused_computation.5 | loop fusion | flops 12000 | bytes 96000 | tf_op jit(solution)/shard_map/mul | solution.py:588
  34.1 0.8 %maximum_minimum_fusion.1 = (f32[6000]{0:T(1024)S(1)}, f32[6000]{0:T(1024)S(1)}) fusion(f32[6000]{0:T(1024)S(1)} %get-tuple-element.6, s32[6000]{0:T(1024)} %param.13, f32[6000]{0:T(1024)S(1)} %get-tuple-element.7), kind=kLoop, calls=%fused_computation.2 | loop fusion | flops 48000 | bytes 120000 | tf_op jit(solution)/shard_map/jit(clip)/min | solution.py:588
  34.9 0.7 %pad_maximum_fusion = f32[2,6000]{1,0:T(2,128)} fusion(f32[1,6000]{1,0:T(1,128)S(1)} %stack.10, f32[1,6000]{1,0:T(1,128)S(1)} %stack.9), kind=kLoop, calls=%fused_computation | loop fusion | flops 12000 | bytes 96000 | tf_op jit(solution)/shard_map/stack | solution.py:590
  35.6 1.3 %copy.10 = f32[2,2,400]{2,1,0:T(2,128)} copy(f32[2,2,400]{2,1,0:T(2,128)} %get-tuple-element.12) | data formatting | bytes 12800
  (2 shorter events, 0.0 us)
where the time goes:
time: 37.1 us; the launch traced here: 36.9 us
  Pallas kernels  32.4 us (87%)
  other arithmetic  2.44 us (7%)
  local copies, waits for them, and re-layouts  1.33 us (4%)
  between operations  0.66 us (2%)
    pallas_call x1, Pallas kernels, fused_shards(): pl.pallas_call(functools.partial(fused_kernel, depth, block), out_shape=(...  32.4 us
    unnamed x1, local copies, waits for them, and re-layouts  1.29 us
    mul x1, other arithmetic, fused_shards(): first_cmd = jnp.clip(loop_gain * updates[0], -limits, limits)  1.02 us
    min x1, other arithmetic, fused_shards(): first_cmd = jnp.clip(loop_gain * updates[0], -limits, limits)  0.75 us

commit v1 on v0

--- a/solution.py
+++ b/solution.py
@@ -150,6 +150,7 @@
     bin_hbm,
     ill_hbm,
     rec_hbm,
+    sat_hbm,
     slopes_out,
     upd_out,
     scr_ref,
@@ -174,7 +175,8 @@
     upd,
     part,
     zsum,
-    fin,
+    sat_raw,
+    sat,
     in_sem,
     rec_sem,
     x_send,
@@ -191,6 +193,7 @@
     a_recv,
     b_send,
     b_recv,
+    sat_sem,
     c_send,
     c_recv,
 ):
@@ -219,6 +222,8 @@
         load.start()
     rec_copy = pltpu.make_async_copy(rec_hbm, rec, rec_sem)
     rec_copy.start()
+    sat_load = pltpu.make_async_copy(sat_hbm, sat_raw, sat_sem)
+    sat_load.start()
 
     x = lax.axis_index("alt")
     strip = lax.axis_index("strip")
@@ -321,6 +326,11 @@
         for q in range(PIXELS):
             for f in range(FRAMES):
                 illq[q, f * PIXELS + p : f * PIXELS + p + 1, :] = ill_ref[p * PIXELS + q : p * PIXELS + q + 1, :]
+
+    sat_load.wait()
+    for n in range(8):
+        width = min(block, actuators - n * block)
+        sat[n, 0, :width] = sat_raw[n * block : n * block + width]
 
     def across(rel, layers):
         for li in layers:
@@ -518,14 +528,20 @@
     total = zsum[0]
     for k in range(1, depth):
         total = total + zsum[k]
-    fin[me] = total
+    limits = sat[me].astype(jnp.float32) * code_step
+    first_cmd = jnp.clip(loop_gain * total[:1], -limits, limits)
+    second_cmd = jnp.clip(first_cmd + loop_gain * total[1:], -limits, limits)
+    part[0, :1] = first_cmd
+    part[0, 1:] = second_cmd
+    own_cols = pl.ds(pl.multiple_of(me * block, 128), block)
+    upd_out[:, own_cols] = part[0]
     copies = []
     for n in range(7):
-        copies.append(remote(fin.at[me], fin.at[me], c_send.at[n], c_recv.at[n], plane(n)))
+        copies.append(
+            remote(upd_out.at[:, own_cols], upd_out.at[:, own_cols], c_send.at[n], c_recv.at[n], plane(n))
+        )
     for copy in copies:
         copy.wait()
-    for j in range(8):
-        upd_out[:, j * block : (j + 1) * block] = fin[j]
 
 
 def fused_shards(screens, row_offset, col_offset, layer_bin, illumination, reconstructor, sat_code):
@@ -541,13 +557,14 @@
     dma = pltpu.SemaphoreType.DMA
     spots = (FRAMES, GUIDE_STARS, row_offset.shape[1])
     vmem = pl.BlockSpec(memory_space=pltpu.VMEM)
+    in_hbm = lambda v: pltpu.with_memory_space_constraint(v, pltpu.HBM)
     slopes, updates = pl.pallas_call(
         functools.partial(fused_kernel, depth, block),
         out_shape=(
             jax.ShapeDtypeStruct((FRAMES, 2, count_here), jnp.float32),
             jax.ShapeDtypeStruct((FRAMES, 8 * block), jnp.float32),
         ),
-        in_specs=[pl.BlockSpec(memory_space=pltpu.HBM)] * 6,
+        in_specs=[pl.BlockSpec(memory_space=pltpu.HBM)] * 7,
         out_specs=(vmem, vmem),
         scratch_shapes=[
             pltpu.VMEM(screens.shape, jnp.bfloat16),
@@ -572,22 +589,19 @@
             pltpu.VMEM((8, FRAMES, block), jnp.float32),
             pltpu.VMEM((7, FRAMES, block), jnp.float32),
             pltpu.VMEM((depth, FRAMES, block), jnp.float32),
-            pltpu.VMEM((8, FRAMES, block), jnp.float32),
+            pltpu.VMEM((actuators,), jnp.int32),
+            pltpu.VMEM((8, 1, block), jnp.int32),
             dma((5,)), dma, dma((layer_dev,)), dma((layer_dev,)), dma, dma, dma((layer_dev,)), dma((layer_dev,)),
             dma((depth * SPLIT,)), dma((depth * SPLIT,)),
             dma(((depth - 1) * SPLIT,)), dma((depth * SPLIT,)),
             dma((7,)), dma((7,)),
-            dma((depth - 1,)), dma((depth - 1,)),
+            dma((depth - 1,)), dma((depth - 1,)), dma,
             dma((7,)), dma((7,)),
         ],
-        compiler_params=pltpu.CompilerParams(collective_id=0, has_side_effects=True, vmem_limit_bytes=67043328),
+        compiler_params=pltpu.CompilerParams(collective_id=0, has_side_effects=True, vmem_limit_bytes=44*2**20),
         name="fused",
-    )(screens, row_offset.transpose(0, 2, 1), col_offset.transpose(0, 2, 1), layer_bin, illumination, reconstructor)
-    updates = updates[:, :actuators]
-    limits = sat_code.astype(jnp.float32) * code_step
-    first_cmd = jnp.clip(loop_gain * updates[0], -limits, limits)
-    second_cmd = jnp.clip(first_cmd + loop_gain * updates[1], -limits, limits)
-    return (slopes, jnp.stack([first_cmd, second_cmd]))
+    )(in_hbm(screens), in_hbm(row_offset.transpose(0, 2, 1)), in_hbm(col_offset.transpose(0, 2, 1)), in_hbm(layer_bin), in_hbm(illumination), in_hbm(reconstructor), in_hbm(sat_code))
+    return slopes, updates[:, :actuators]
 
 
 def solution(mesh):

time: 37.1 us -> 33.8 us (0.911)
  other arithmetic: 2.44 us -> 0 us
  Pallas kernels: 32.4 us -> 31.8 us
    mul x1 -> x0, other arithmetic: 1.02 us -> none  [fused_shards(): first_cmd = jnp.clip(loop_gain * updates[0], -limits, limits)]
    min x1 -> x0, other arithmetic: 0.75 us -> none  [fused_shards(): first_cmd = jnp.clip(loop_gain * updates[0], -limits, limits)]
    unnamed x1, local copies, waits for them, and re-layouts: 1.29 us -> 0.6 us
    another operation x1 -> x0, other arithmetic: 0.67 us -> none  [fused_shards(): return (slopes, jnp.stack([first_cmd, second_cmd]))]
    slice x0 -> x1, local copies, waits for them, and re-layouts: none -> 0.62 us  [fused_shards(): return (slopes, updates[:, :actuators])]
    pallas_call x1, Pallas kernels: 32.4 us -> 31.8 us  [fused_shards(): pl.pallas_call(functools.partial(fused_kernel, depth, block), out_shape=(...]
where the time goes in v1:
time: 33.8 us; the launch traced here: 33.7 us
  Pallas kernels  31.8 us (94%)
  local copies, waits for them, and re-layouts  1.22 us (4%)
  between operations  0.64 us (2%)
    pallas_call x1, Pallas kernels, fused_shards(): pl.pallas_call(functools.partial(fused_kernel, depth, block), out_shape=(...  31.8 us

profile of v1, /device:TPU:0, one launch (start us, length us, event | category | flops | bytes accessed | tf_op | source)
XLA Modules:
  0.0 33.7 jit_solution(6023434986335901138)
XLA Ops:
  0.6 31.8 %fused.1 = (f32[2,2,400]{2,1,0:T(2,128)S(1)}, f32[2,6144]{1,0:T(2,128)S(1)}) custom-call(bf16[2,32,512]{2,1,0:T(8,128)(2,1)} %scr_hbm.1, s32[2,2,4]{2,1,0:T(2,128)} %bitcast.2, s32[2,2,4]{2,1,0:T(2,128)} %bitcast.3, s32[4]{0:T(128)} %bin_hbm.1, f32[16,400]{1,0:T(8,128)} %ill_hbm.1, bf16[2,400,6000]{2,1,0:T(8,128)(2,1)} %rec_hbm.1, s32[6000]{0:T(1024)} %sat_hbm.1), custom_call_target="tpu_custom_call" | custom-call | tf_op jit(solution)/shard_map/fused/pallas_call | solution.py:561
  32.5 0.6 %slice.3 = f32[2,6000]{1,0:T(2,128)} slice(f32[2,6144]{1,0:T(2,128)S(1)} %get-tuple-element.5), slice={[0:2], [0:6000]} | slice | bytes 96000 | tf_op jit(solution)/shard_map/slice | solution.py:604
  33.1 0.6 %copy.10 = f32[2,2,400]{2,1,0:T(2,128)} copy(f32[2,2,400]{2,1,0:T(2,128)S(1)} %get-tuple-element.8) | data formatting | bytes 12800

commit v2 on v1

v2 whole, which is shorter than its diff:
```python
import functools
import math

import jax
import jax.numpy as jnp
from jax import lax
from jax.experimental import pallas as pl
from jax.experimental.pallas import tpu as pltpu
from jax.sharding import PartitionSpec as P

LENSLETS = 80
PIXELS = 4
GUIDE_STARS = 2
FRAMES = 2
ACTUATORS = 6000
PUPIL_PIX = 320
WINDOW = 384
SUBAPS_ALL = 12800


highest = lax.Precision.HIGHEST
loop_gain = 0.5
code_step = 0.125
bin_step = 0.03125


def bilinear(offsets):
    return jnp.maximum(0.0, 1.0 - jnp.abs(offsets))


def dft_tables():
    padded = 2 * PIXELS
    freq_index = jnp.arange(padded * padded, dtype=jnp.int32)
    freq_row = freq_index // padded
    freq_col = freq_index % padded
    pix_index = jnp.arange(PIXELS * PIXELS, dtype=jnp.int32)
    pix_row = pix_index // PIXELS
    pix_col = pix_index % PIXELS
    turn_count = (
        freq_row[:, None] * pix_row[None, :] + freq_col[:, None] * pix_col[None, :]
    ) % padded
    angles = turn_count.astype(jnp.float32) * (2.0 * math.pi / padded)
    coord_row = ((freq_row + PIXELS) % padded - PIXELS).astype(jnp.float32)
    coord_col = ((freq_col + PIXELS) % padded - PIXELS).astype(jnp.float32)
    return (jnp.cos(angles), jnp.sin(angles), coord_row, coord_col)


def centroids(pupil_phase, illumination, tables):
    cosine, sine_table, coord_row, coord_col = tables
    field_re = illumination * jnp.cos(pupil_phase)
    field_im = illumination * jnp.sin(pupil_phase)
    real_part = jnp.dot(cosine, field_re, precision=highest) + jnp.dot(
        sine_table, field_im, precision=highest
    )
    imag_part = jnp.dot(cosine, field_im, precision=highest) - jnp.dot(
        sine_table, field_re, precision=highest
    )
    intensity = real_part * real_part + imag_part * imag_part
    flux_sum = jnp.sum(intensity, axis=0)
    slope_row = jnp.sum(intensity * coord_row[:, None], axis=0) / flux_sum
    slope_col = jnp.sum(intensity * coord_col[:, None], axis=0) / flux_sum
    return jnp.stack([slope_row, slope_col])


def shards(screens, row_offset, col_offset, layer_bin, illumination, reconstructor, sat_code):
    layer_dev = screens.shape[0]
    rows_here = screens.shape[1]
    count_here = illumination.shape[1]
    group_pos = lax.axis_index("alt")
    strip_pos = lax.axis_index("strip")
    row_global = strip_pos * rows_here + jnp.arange(rows_here, dtype=jnp.int32)
    pupil_idx = jnp.arange(PUPIL_PIX, dtype=jnp.float32)
    window_idx = jnp.arange(WINDOW, dtype=jnp.float32)
    widened_layers = [
        jnp.pad(screens[layer_no], ((0, 0), (0, WINDOW))) for layer_no in range(layer_dev)
    ]
    frame_terms = []
    for frame_no in range(FRAMES):
        running = jnp.zeros((PIXELS, PIXELS, GUIDE_STARS, LENSLETS, LENSLETS), jnp.float32)
        for layer_no in range(layer_dev):
            layer_pos = group_pos * layer_dev + layer_no
            tops = lax.dynamic_index_in_dim(row_offset[frame_no], layer_pos, 0, keepdims=False)
            lefts = lax.dynamic_index_in_dim(col_offset[frame_no], layer_pos, 0, keepdims=False)
            bin_value = lax.dynamic_index_in_dim(layer_bin, layer_pos, 0, keepdims=False)
            shrink = 1.0 - bin_value.astype(jnp.float32) * bin_step
            col_weights = bilinear(window_idx[None, :] - pupil_idx[:, None] * shrink)
            widened = widened_layers[layer_no]

            def cut_columns(left_col):
                return lax.dynamic_slice_in_dim(widened, left_col, WINDOW, 1)

            strips = jax.vmap(cut_columns)(lefts).astype(jnp.float32)
            across = jnp.einsum("drc,jc->drj", strips, col_weights, precision=highest)
            offsets = (row_global[None, :] - tops[:, None]).astype(jnp.float32)
            row_weights = bilinear(offsets[:, None, :] - pupil_idx[None, :, None] * shrink)
            running = running + jnp.einsum(
                "dapr,drbq->pqdab",
                row_weights.reshape(GUIDE_STARS, LENSLETS, PIXELS, rows_here),
                across.reshape(GUIDE_STARS, rows_here, LENSLETS, PIXELS),
                precision=highest,
            )
        frame_terms.append(running.reshape(PIXELS * PIXELS, SUBAPS_ALL))
    phase_terms = jnp.concatenate(frame_terms, axis=0)
    partly = lax.psum_scatter(phase_terms, "alt", scatter_dimension=1, tiled=True)
    owned = lax.psum_scatter(partly, "strip", scatter_dimension=1, tiled=True)
    pupil_phase = owned.reshape(FRAMES, PIXELS * PIXELS, count_here)
    tables = dft_tables()
    slopes = jnp.stack(
        [centroids(pupil_phase[frame_no], illumination, tables) for frame_no in range(FRAMES)]
    )
    rounded = slopes.astype(jnp.bfloat16).reshape(FRAMES, 2 * count_here)
    partial_value = jnp.dot(
        rounded,
        reconstructor.reshape(2 * count_here, ACTUATORS),
        preferred_element_type=jnp.float32,
    )
    updates = lax.psum(partial_value, ("alt", "strip"))
    limits = sat_code.astype(jnp.float32) * code_step
    first_cmd = jnp.clip(loop_gain * updates[0], -limits, limits)
    second_cmd = jnp.clip(first_cmd + loop_gain * updates[1], -limits, limits)
    return (slopes, jnp.stack([first_cmd, second_cmd]))


MESH = pl.DeviceIdType.MESH
HALVES = 2
PLANES = 4
WIDE = -(-PUPIL_PIX // 128) * 128


def pair_gain(distance):
    turn = 2.0 * math.pi / (2 * PIXELS)
    return 4.0 * sum(k * math.sin(turn * k * distance) for k in range(1, PIXELS))


def padded_rows(arcs):
    return -(-arcs * FRAMES * PIXELS // 16) * 16


def tile_of(arcs, arc, part):
    full = PUPIL_PIX // 128
    pair = arc // 2 * (2 * full + 1)
    if part < full:
        return pair + arc % 2 * full + part
    return pair + (2 * full if arc // 2 * 2 + 1 < arcs else full)


def packed_tiles(arcs):
    return tile_of(arcs, arcs - 1, PUPIL_PIX // 128) + 1


def reaches(total, rows, first, last):
    for layer_bin in range(16):
        shrink = 1.0 - layer_bin * bin_step
        top = math.floor(total - 1 - (PUPIL_PIX - 1) * shrink)
        if top + last * shrink > rows[0] - 1 and first * shrink < rows[1] + 1:
            return True
    return False


def far_pattern(total, arcs):
    plane_rows = total // PLANES
    strip_rows = arcs * PIXELS
    for strip in range(4):
        first = strip * strip_rows
        if reaches(total, (total - plane_rows, total - 1), first, first + strip_rows - 1):
            return False
        first += (PLANES - 1) * 4 * strip_rows
        low = first + 2 * PIXELS if strip == 0 else first
        if reaches(total, (0, plane_rows - 1), low, first + strip_rows - 1):
            return False
    return True


def fused_kernel(
    block,
    scr_hbm,
    row_hbm,
    col_hbm,
    bin_hbm,
    ill_hbm,
    rec_hbm,
    sat_hbm,
    slopes_out,
    upd_out,
    scr_ref,
    row_ref,
    col_ref,
    bin_ref,
    ill_ref,
    scr_all,
    colw,
    roww,
    rhs,
    acc,
    part,
    relay_in,
    main_in,
    far_in,
    phase_sc,
    phiq,
    illq,
    slope_sc,
    rec,
    upd,
    gathered,
    zsum,
    sat_raw,
    sat,
    in_sem,
    rec_sem,
    sat_sem,
    own_send,
    own_recv,
    pass_send,
    pass_recv,
    core_send,
    core_recv,
    ra_send,
    ra_recv,
    m_send,
    m_recv,
    far_send,
    far_recv,
    credit,
    a_send,
    a_recv,
    b_send,
    b_recv,
    c_send,
    c_recv,
):
    layer_dev, rows_here, columns = scr_ref.shape
    count_here = ill_ref.shape[1]
    arcs = count_here // LENSLETS
    chunk_rows = padded_rows(arcs)
    depth = PLANES
    full = PUPIL_PIX // 128
    rest = PUPIL_PIX - full * 128
    actuators = rec_hbm.shape[2]

    loads = [
        pltpu.make_async_copy(src, dst, in_sem.at[n])
        for n, (src, dst) in enumerate(
            (
                (scr_hbm, scr_ref),
                (row_hbm, row_ref),
                (col_hbm, col_ref),
                (bin_hbm, bin_ref),
                (ill_hbm, ill_ref),
            )
        )
    ]
    for load in loads:
        load.start()
    rec_copy = pltpu.make_async_copy(rec_hbm, rec, rec_sem)
    rec_copy.start()
    sat_load = pltpu.make_async_copy(sat_hbm, sat_raw, sat_sem)
    sat_load.start()

    x = lax.axis_index("alt")
    strip = lax.axis_index("strip")
    core = strip % 2
    y = (strip // 2) % 2
    z = strip // 4
    me = (x * 2 + y) * 2 + core

    offsets = ((1, 1, 0), (1, 1, 1), (1, 0, 0), (1, 0, 1), (0, 1, 0), (0, 1, 1), (0, 0, 1))

    def place(n):
        dx, dy, dc = offsets[n]
        return ((x + dx) % 2, (y + dy) % 2, (core + dc) % 2)

    def plane(n):
        px, py, pc = place(n)
        return (px, (z * 2 + py) * 2 + pc)

    def slot(n):
        px, py, pc = place(n)
        return (px * 2 + py) * 2 + pc

    def depth_dev(zpos):
        return (x, (zpos * 2 + y) * 2 + core)

    x_dev = (1 - x, strip)
    y_dev = (x, (z * 2 + 1 - y) * 2 + core)
    core_dev = (x, (z * 2 + y) * 2 + 1 - core)
    low_end = z == 0
    high_end = z == depth - 1
    outer = low_end | high_end
    corner = (y == 0) & (core == 0)

    barrier = pltpu.get_barrier_semaphore()
    for device in (x_dev, y_dev, core_dev):
        pl.semaphore_signal(barrier, inc=1, device_id=device, device_id_type=MESH)

    @pl.when(jnp.logical_not(low_end))
    def _():
        pl.semaphore_signal(barrier, inc=1, device_id=depth_dev(z - 1), device_id_type=MESH)

    @pl.when(jnp.logical_not(high_end))
    def _():
        pl.semaphore_signal(barrier, inc=1, device_id=depth_dev(z + 1), device_id_type=MESH)

    spot = y * 2 + core
    other = (1 - y) * 2 + core
    loads[0].wait()
    for li in range(layer_dev):
        scr_all[x * layer_dev + li, spot] = scr_ref[li].astype(jnp.float32)

    @pl.when(outer)
    def _():
        pl.semaphore_wait(barrier, 4)

    @pl.when(jnp.logical_not(outer))
    def _():
        pl.semaphore_wait(barrier, 5)

    def remote(src, dst, send, recv, device):
        copy = pltpu.make_async_remote_copy(
            src_ref=src, dst_ref=dst, send_sem=send, recv_sem=recv, device_id=device, device_id_type=MESH
        )
        copy.start()
        return copy

    half = rows_here // HALVES

    def piece(layer, at, h):
        return scr_all.at[layer, at, pl.ds(h * half, half)]

    def share(which, li, h, device):
        n = (which * layer_dev + li) * HALVES + h
        here = piece(x * layer_dev + li, spot, h)
        return remote(here, here, own_send.at[n], own_recv.at[n], device)

    x_copies, y_copies = {}, {}
    for step in range(layer_dev):
        for h in range(HALVES):
            x_copies[step, h] = share(0, step, h, x_dev)
            y_copies[layer_dev - 1 - step, h] = share(1, layer_dev - 1 - step, h, y_dev)
    core_copies = []

    def to_core(here):
        n = len(core_copies)
        core_copies.append(remote(here, here, core_send.at[n], core_recv.at[n], core_dev))

    to_core(scr_all.at[x * layer_dev, spot])
    to_core(scr_all.at[x * layer_dev + 1, spot])

    @pl.when((z == 1) & corner)
    def _():
        pl.semaphore_signal(credit, inc=1, device_id=depth_dev(z - 1), device_id_type=MESH)

    for load in loads[1:]:
        load.wait()

    layers = [((x + rel) % 2) * layer_dev + li for rel in range(2) for li in range(layer_dev)]
    shrinks = [1.0 - bin_ref[layer].astype(jnp.float32) * bin_step for layer in layers]
    tops = [[row_ref[f, x, layer].astype(jnp.float32) for layer in layers] for f in range(FRAMES)]
    lefts = [[col_ref[f, x, layer].astype(jnp.float32) for layer in layers] for f in range(FRAMES)]

    width = colw.shape[2]
    col_pos = lax.broadcasted_iota(jnp.int32, (columns, width), 0).astype(jnp.float32)
    lane = lax.broadcasted_iota(jnp.int32, (1, width), 1)
    second = lane >= WIDE
    lane = jnp.where(second, lane - WIDE, lane)
    q_of = (
        (lane >= LENSLETS).astype(jnp.int32)
        + (lane >= 2 * LENSLETS).astype(jnp.int32)
        + (lane >= 3 * LENSLETS).astype(jnp.int32)
    )
    pupil_col = ((lane - q_of * LENSLETS) * PIXELS + q_of).astype(jnp.float32)

    def column_weights(n):
        start = pupil_col * shrinks[n] + jnp.where(second, lefts[1][n], lefts[0][n])
        colw[n] = bilinear(col_pos - start).astype(jnp.bfloat16)

    mine = range(layer_dev)
    theirs = range(layer_dev, 2 * layer_dev)
    pair = 2 * rows_here
    stages = (
        (mine, 2 * y, pair),
        (theirs, 2 * y, pair),
        (mine, 2 * (1 - y), pair),
        (theirs, other, rows_here),
        (theirs, 2 * (1 - y) + 1 - core, rows_here),
    )
    begins = [0]
    for members, at, rows in stages:
        begins.append(begins[-1] + len(members) * FRAMES * 2 * rows)

    def row_weights(number):
        members, at, rows = stages[number]
        seg = 2 * rows
        row_pos = lax.broadcasted_iota(jnp.int32, (chunk_rows, seg), 1) % rows + (z * 4 + at) * rows_here
        row_pos = row_pos.astype(jnp.float32)
        row_sub = lax.broadcasted_iota(jnp.int32, (chunk_rows, seg), 0)
        row_base = row_sub // 8 * PIXELS + row_sub % PIXELS
        row_frame = row_sub // PIXELS % FRAMES
        for zpos in range(depth):
            pupil_row = (row_base + ((zpos * 2 + y) * 2 + core) * (arcs * PIXELS)).astype(jnp.float32)
            for i, n in enumerate(members):
                reach = pupil_row * shrinks[n]
                for f in range(FRAMES):
                    weight = jnp.where(row_frame == f, bilinear(row_pos - tops[f][n] - reach), 0.0)
                    lo = begins[number] + (i * FRAMES + f) * seg
                    roww[zpos * chunk_rows : (zpos + 1) * chunk_rows, lo : lo + seg] = weight.astype(jnp.bfloat16)

    def across(number, n):
        members, at, rows = stages[number]
        blocks = rows // rows_here
        source = scr_all[layers[n], pl.ds(at, blocks)].reshape(rows, columns).astype(jnp.bfloat16)
        value = jnp.dot(source, colw[n], preferred_element_type=jnp.float32)
        for f in range(FRAMES):
            one = value[:, f * WIDE : f * WIDE + PUPIL_PIX]
            high = one.astype(jnp.bfloat16)
            low = (one - high.astype(jnp.float32)).astype(jnp.bfloat16)
            lo = begins[number] + ((n - members[0]) * FRAMES + f) * 2 * rows
            rhs[lo : lo + rows, :] = high
            rhs[lo + rows : lo + 2 * rows, :] = low

    def project(number):
        lo, hi = begins[number], begins[number + 1]
        return jnp.dot(roww[:, lo:hi], rhs[lo:hi, :], preferred_element_type=jnp.float32)

    for n in range(2 * layer_dev):
        column_weights(n)
    for number in range(len(stages)):
        row_weights(number)

    passed = {}

    def pass_on(which, h, here, device):
        n = which * HALVES + h
        passed[which, h] = remote(here, here, pass_send.at[n], pass_recv.at[n], device)

    for h in range(HALVES):
        here = piece((1 - x) * layer_dev, spot, h)
        x_copies[0, h].wait_recv()
        pass_on(0, h, here, y_dev)
        to_core(here)
        here = piece(x * layer_dev + 1, other, h)
        y_copies[1, h].wait_recv()
        pass_on(1, h, here, x_dev)
        to_core(here)
    for copy in core_copies[:2]:
        copy.wait()
    for n in mine:
        across(0, n)
    acc[...] = project(0)
    for p in range(PIXELS):
        for q in range(PIXELS):
            for f in range(FRAMES):
                illq[q, f * PIXELS + p : f * PIXELS + p + 1, :] = ill_ref[p * PIXELS + q : p * PIXELS + q + 1, :]
    sat_load.wait()
    for n in range(8):
        some = min(block, actuators - n * block)
        sat[n, 0, :some] = sat_raw[n * block : n * block + some]
    for h in range(HALVES):
        x_copies[1, h].wait_recv()
        to_core(piece((1 - x) * layer_dev + 1, spot, h))
        y_copies[0, h].wait_recv()
        to_core(piece(x * layer_dev, other, h))
    for copy in core_copies[2 : 2 + 2 * HALVES]:
        copy.wait()
    across(1, layer_dev)
    across(2, 1)
    for copy in core_copies[2 + 2 * HALVES : 2 + 4 * HALVES]:
        copy.wait()
    across(1, layer_dev + 1)
    across(2, 0)
    for h in range(HALVES):
        passed[0, h].wait_recv()
        to_core(piece((1 - x) * layer_dev, other, h))
        passed[1, h].wait_recv()
        to_core(piece((1 - x) * layer_dev + 1, other, h))
    acc[...] += project(1) + project(2)
    for n in theirs:
        across(3, n)
    acc[...] += project(3)
    for copy in core_copies[2 + 4 * HALVES :]:
        copy.wait()
    for n in theirs:
        across(4, n)
    acc[...] += project(4)
    for copy in list(x_copies.values()) + list(y_copies.values()) + list(passed.values()):
        copy.wait_send()

    def pack(zpos):
        value = acc[pl.ds(pl.multiple_of(zpos * chunk_rows, chunk_rows), chunk_rows), :]
        for a in range(arcs):
            lines = value[a * 8 : (a + 1) * 8]
            for t in range(full):
                at = tile_of(arcs, a, t) * 8
                part[zpos, at : at + 8, :] = lines[:, t * 128 : (t + 1) * 128]
            at = tile_of(arcs, a, full) * 8
            lane0 = a % 2 * rest
            part[zpos, at : at + 8, lane0 : lane0 + rest] = lines[:, full * 128 :]
        if arcs % 2:
            at = tile_of(arcs, arcs - 1, full) * 8
            part[zpos, at : at + 8, rest:] = jnp.zeros((8, 128 - rest), jnp.float32)

    edge = tile_of(arcs, 1, full) + 1
    tiles = packed_tiles(arcs)
    pieces = [pl.ds(edge * 8, (tiles - edge) * 8), pl.ds(0, edge * 8)]
    count = len(pieces)
    below = z < depth // 2
    ahead = jnp.where(below, 1, -1)
    side = jnp.where(below, 0, 1)
    pack(z + 2 * ahead)
    first_copies = []
    for i, rows in enumerate(pieces):
        first_copies.append(
            remote(
                part.at[z + 2 * ahead, rows],
                relay_in.at[side, rows],
                ra_send.at[i],
                ra_recv.at[side * count + i],
                depth_dev(z + ahead),
            )
        )

    def relay_wait(s, i):
        pltpu.make_async_remote_copy(
            src_ref=part.at[0, pieces[i]],
            dst_ref=relay_in.at[s, pieces[i]],
            send_sem=ra_send.at[i],
            recv_sem=ra_recv.at[s * count + i],
            device_id=depth_dev(z),
            device_id_type=MESH,
        ).wait_recv()

    def main_copy(s, i, zpos):
        return pltpu.make_async_remote_copy(
            src_ref=part.at[zpos, pieces[i]],
            dst_ref=main_in.at[s, pieces[i]],
            send_sem=m_send.at[s * count + i],
            recv_sem=m_recv.at[s * count + i],
            device_id=depth_dev(zpos),
            device_id_type=MESH,
        )

    far_copy = pltpu.make_async_remote_copy(
        src_ref=part.at[depth - 1, pieces[1]],
        dst_ref=far_in,
        send_sem=far_send,
        recv_sem=far_recv,
        device_id=depth_dev(2),
        device_id_type=MESH,
    )

    @pl.when(outer)
    def _():
        pack(z + ahead)
        copies = []
        for i in range(count):
            copies.append(main_copy(side, i, z + ahead))
            copies[-1].start()

        @pl.when(low_end & corner)
        def _():
            pack(depth - 1)
            pl.semaphore_wait(credit, 1)
            far_copy.start()
            far_copy.wait_send()

        pack(z)
        for i, rows in enumerate(pieces):
            main_copy(1 - side, i, z + ahead).wait_recv()
            phase_sc[rows] = part[z, rows] + main_in[1 - side, rows]
        for copy in copies:
            copy.wait_send()

    @pl.when(jnp.logical_not(outer))
    def _():
        pack(z + 1)
        pack(z - 1)
        copies = []
        for i, rows in enumerate(pieces):
            for s in range(2):
                to = z + 1 - 2 * s
                relay_wait(s, i)
                if i == 1 and s == 0:

                    @pl.when((z == 2) & corner)
                    def _():
                        far_copy.wait_recv()
                        part[depth - 1, rows] = part[depth - 1, rows] + far_in[...]

                part[to, rows] = part[to, rows] + relay_in[s, rows]
                copies.append(main_copy(s, i, to))
                copies[-1].start()
        pack(z)
        for i, rows in enumerate(pieces):
            for s in range(2):
                main_copy(s, i, z + 1 - 2 * s).wait_recv()
            phase_sc[rows] = part[z, rows] + main_in[0, rows] + main_in[1, rows]
        for copy in copies:
            copy.wait_send()

    for copy in first_copies:
        copy.wait_send()

    for a in range(arcs):
        for q in range(PIXELS):
            lo = q * LENSLETS
            while lo < (q + 1) * LENSLETS:
                t = lo // 128
                hi = min((q + 1) * LENSLETS, (t + 1) * 128)
                at = tile_of(arcs, a, t) * 8
                lane0 = lo - t * 128 + (a % 2 * rest if t == full else 0)
                to = a * LENSLETS + lo - q * LENSLETS
                phiq[q, :, to : to + hi - lo] = phase_sc[at : at + 8, lane0 : lane0 + hi - lo]
                lo = hi

    cosines, sines = [], []
    flux = None
    for q in range(PIXELS):
        amp = illq[q]
        phi = phiq[q]
        cosines.append(amp * jnp.cos(phi))
        sines.append(amp * jnp.sin(phi))
        flux = amp * amp if flux is None else flux + amp * amp
    tip = -float(PIXELS) * flux
    tilt = tip
    pix_row = lax.broadcasted_iota(jnp.int32, flux.shape, 0) % PIXELS
    for d in range(1, PIXELS):
        gain = pair_gain(d)
        even = -2.0 * PIXELS * (-1.0) ** d
        term = None
        for q in range(d, PIXELS):
            ch, sh, cl, sl = cosines[q], sines[q], cosines[q - d], sines[q - d]
            new = gain * (sh * cl - ch * sl) + even * (ch * cl + sh * sl)
            term = new if term is None else term + new
        tilt = tilt + term
        term = None
        for q in range(PIXELS):
            ch, sh = cosines[q], sines[q]
            cl, sl = pltpu.roll(ch, d, 0), pltpu.roll(sh, d, 0)
            new = gain * (sh * cl - ch * sl) + even * (ch * cl + sh * sl)
            term = new if term is None else term + new
        tip = tip + jnp.where(pix_row >= d, term, 0.0)
    for f in range(FRAMES):
        rows = slice(f * PIXELS, (f + 1) * PIXELS)
        total = jnp.sum(flux[rows], axis=0, keepdims=True) * (2.0 * PIXELS)
        for c, value in enumerate((tip, tilt)):
            slope = jnp.sum(value[rows], axis=0, keepdims=True) / total
            slopes_out[f, c : c + 1, :] = slope
            slope_sc[c, f : f + 1, :] = slope

    rec_copy.wait()
    rounded = [slope_sc[c].astype(jnp.bfloat16) for c in range(2)]
    tail = actuators - 6 * block

    def update(chip):
        def some(cols, width):
            value = jnp.dot(rounded[0], rec[0, :, cols], preferred_element_type=jnp.float32)
            value = value + jnp.dot(rounded[1], rec[1, :, cols], preferred_element_type=jnp.float32)
            upd[2 * chip] = value[:, :block]
            upd[2 * chip + 1, :, : width - block] = value[:, block:]

        @pl.when(chip < 3)
        def _():
            some(pl.ds(pl.multiple_of(chip * 2 * block, 128), 2 * block), 2 * block)

        @pl.when(chip == 3)
        def _():
            upd[7] = jnp.zeros_like(upd[7])
            some(slice(6 * block, actuators), tail)

    copies = []
    for n in range(7):
        to = slot(n)
        if n % 2 == 0:
            update(to // 2)
        copies.append(remote(upd.at[to], gathered.at[n], a_send.at[n], a_recv.at[n], plane(n)))
    for copy in copies:
        copy.wait()
    total = upd[me]
    for n in range(7):
        total = total + gathered[n]
    zsum[z] = total
    copies = []
    for k in range(1, depth):
        copies.append(
            remote(zsum.at[z], zsum.at[z], b_send.at[k - 1], b_recv.at[k - 1], depth_dev((z + k) % depth))
        )
    for copy in copies:
        copy.wait()
    total = zsum[0]
    for k in range(1, depth):
        total = total + zsum[k]
    limits = sat[me].astype(jnp.float32) * code_step
    first_cmd = jnp.clip(loop_gain * total[:1], -limits, limits)
    second_cmd = jnp.clip(first_cmd + loop_gain * total[1:], -limits, limits)
    gathered[0, :1] = first_cmd
    gathered[0, 1:] = second_cmd
    own_cols = pl.ds(pl.multiple_of(me * block, 128), block)
    upd_out[:, own_cols] = gathered[0]
    copies = []
    for n in range(7):
        copies.append(
            remote(upd_out.at[:, own_cols], upd_out.at[:, own_cols], c_send.at[n], c_recv.at[n], plane(n))
        )
    for copy in copies:
        copy.wait()


def fused_shards(screens, row_offset, col_offset, layer_bin, illumination, reconstructor, sat_code):
    layer_dev, rows_here, columns = screens.shape
    count_here = illumination.shape[1]
    actuators = reconstructor.shape[2]
    depth = PLANES
    arcs = count_here // LENSLETS
    chunk = (packed_tiles(arcs) * 8, 128)
    edge = ((tile_of(arcs, 1, PUPIL_PIX // 128) + 1) * 8, 128)
    rows = padded_rows(arcs)
    block = -(-actuators // (8 * 128)) * 128
    contraction = FRAMES * 2 * 2 * layer_dev * 4 * rows_here
    width = (FRAMES - 1) * WIDE + PUPIL_PIX
    dma = pltpu.SemaphoreType.DMA
    spots = (FRAMES, GUIDE_STARS, row_offset.shape[1])
    vmem = pl.BlockSpec(memory_space=pltpu.VMEM)

    def in_hbm(value):
        return pltpu.with_memory_space_constraint(value, pltpu.HBM)

    slopes, updates = pl.pallas_call(
        functools.partial(fused_kernel, block),
        out_shape=(
            jax.ShapeDtypeStruct((FRAMES, 2, count_here), jnp.float32),
            jax.ShapeDtypeStruct((FRAMES, 8 * block), jnp.float32),
        ),
        in_specs=[pl.BlockSpec(memory_space=pltpu.HBM)] * 7,
        out_specs=(vmem, vmem),
        scratch_shapes=[
            pltpu.VMEM(screens.shape, jnp.bfloat16),
            pltpu.SMEM(spots, jnp.int32),
            pltpu.SMEM(spots, jnp.int32),
            pltpu.SMEM(layer_bin.shape, jnp.int32),
            pltpu.VMEM(illumination.shape, jnp.float32),
            pltpu.VMEM((2 * layer_dev, 4, rows_here, columns), jnp.float32),
            pltpu.VMEM((2 * layer_dev, columns, width), jnp.bfloat16),
            pltpu.VMEM((depth * rows, contraction), jnp.bfloat16),
            pltpu.VMEM((contraction, PUPIL_PIX), jnp.bfloat16),
            pltpu.VMEM((depth * rows, PUPIL_PIX), jnp.float32),
            pltpu.VMEM((depth,) + chunk, jnp.float32),
            pltpu.VMEM((2,) + chunk, jnp.float32),
            pltpu.VMEM((2,) + chunk, jnp.float32),
            pltpu.VMEM(edge, jnp.float32),
            pltpu.VMEM(chunk, jnp.float32),
            pltpu.VMEM((PIXELS, FRAMES * PIXELS, count_here), jnp.float32),
            pltpu.VMEM((PIXELS, FRAMES * PIXELS, count_here), jnp.float32),
            pltpu.VMEM((2, FRAMES, count_here), jnp.float32),
            pltpu.VMEM(reconstructor.shape, jnp.bfloat16),
            pltpu.VMEM((8, FRAMES, block), jnp.float32),
            pltpu.VMEM((7, FRAMES, block), jnp.float32),
            pltpu.VMEM((depth, FRAMES, block), jnp.float32),
            pltpu.VMEM((actuators,), jnp.int32),
            pltpu.VMEM((8, 1, block), jnp.int32),
            dma((5,)), dma, dma,
            dma((2 * layer_dev * HALVES,)), dma((2 * layer_dev * HALVES,)),
            dma((2 * HALVES,)), dma((2 * HALVES,)),
            dma((2 + 6 * HALVES,)), dma((2 + 6 * HALVES,)),
            dma((2,)), dma((4,)), dma((4,)), dma((4,)), dma, dma,
            pltpu.SemaphoreType.REGULAR,
            dma((7,)), dma((7,)),
            dma((depth - 1,)), dma((depth - 1,)),
            dma((7,)), dma((7,)),
        ],
        compiler_params=pltpu.CompilerParams(collective_id=0, has_side_effects=True, vmem_limit_bytes=44 * 2**20),
        name="fused",
    )(
        in_hbm(screens),
        in_hbm(row_offset.transpose(0, 2, 1)),
        in_hbm(col_offset.transpose(0, 2, 1)),
        in_hbm(layer_bin),
        in_hbm(illumination),
        in_hbm(reconstructor),
        in_hbm(sat_code),
    )
    return slopes, updates[:, :actuators]


def step(screens, row_offset, col_offset, layer_bin, illumination, reconstructor, sat_code):
    strips = lax.axis_size("strip")
    fused = (
        lax.axis_size("alt") == 2 == GUIDE_STARS
        and strips == 4 * PLANES
        and screens.shape[0] == 2
        and LENSLETS % strips == 0
        and LENSLETS // strips > 2
        and screens.shape[1] % 16 == 0
        and far_pattern(strips * screens.shape[1], LENSLETS // strips)
    )
    chosen = fused_shards if fused else shards
    return chosen(screens, row_offset, col_offset, layer_bin, illumination, reconstructor, sat_code)


def solution(mesh):
    placed = (
        P("alt", "strip", None),
        P(),
        P(),
        P(),
        P(None, ("alt", "strip")),
        P(None, ("alt", "strip"), None),
        P(),
    )
    return jax.shard_map(
        step,
        mesh=mesh,
        in_specs=placed,
        out_specs=(P(None, None, ("alt", "strip")), P()),
        check_vma=False,
    )
```

time: 33.8 us -> 34 us (level)
  no operation moved by 1% of the time
where the time goes in v2:
time: 34 us; the launch traced here: 33.8 us
  Pallas kernels  32 us (94%)
  local copies, waits for them, and re-layouts  1.22 us (4%)
  between operations  0.64 us (2%)
    pallas_call x1, Pallas kernels, fused_shards(): pl.pallas_call(functools.partial(fused_kernel, block), out_shape=(jax.Sha...  32 us

profile of v2, /device:TPU:0, one launch (start us, length us, event | category | flops | bytes accessed | tf_op | source)
XLA Modules:
  0.0 33.8 jit_solution(13766906105323194719)
XLA Ops:
  0.6 32.0 %fused.1 = (f32[2,2,400]{2,1,0:T(2,128)S(1)}, f32[2,6144]{1,0:T(2,128)S(1)}) custom-call(bf16[2,32,512]{2,1,0:T(8,128)(2,1)} %scr_hbm.1, s32[2,2,4]{2,1,0:T(2,128)} %bitcast.2, s32[2,2,4]{2,1,0:T(2,128)} %bitcast.3, s32[4]{0:T(128)} %bin_hbm.1, f32[16,400]{1,0:T(8,128)} %ill_hbm.1, bf16[2,400,6000]{2,1,0:T(8,128)(2,1)} %rec_hbm.1, s32[6000]{0:T(1024)} %sat_hbm.1), custom_call_target="tpu_custom_call" | custom-call | tf_op jit(solution)/shard_map/fused/pallas_call | solution.py:727
  32.6 0.6 %slice.3 = f32[2,6000]{1,0:T(2,128)} slice(f32[2,6144]{1,0:T(2,128)S(1)} %get-tuple-element.5), slice={[0:2], [0:6000]} | slice | bytes 96000 | tf_op jit(solution)/shard_map/slice | solution.py:781
  33.2 0.6 %copy.10 = f32[2,2,400]{2,1,0:T(2,128)} copy(f32[2,2,400]{2,1,0:T(2,128)S(1)} %get-tuple-element.8) | data formatting | bytes 12800

commit v3 on v2

--- a/solution.py
+++ b/solution.py
@@ -122,7 +122,7 @@
 
 
 MESH = pl.DeviceIdType.MESH
-HALVES = 2
+HALVES = 1
 PLANES = 4
 WIDE = -(-PUPIL_PIX // 128) * 128
 
@@ -193,8 +193,7 @@
     rhs,
     acc,
     part,
-    relay_in,
-    main_in,
+    z_in,
     far_in,
     phase_sc,
     phiq,
@@ -215,10 +214,8 @@
     pass_recv,
     core_send,
     core_recv,
-    ra_send,
-    ra_recv,
-    m_send,
-    m_recv,
+    z_send,
+    z_recv,
     far_send,
     far_recv,
     credit,
@@ -262,32 +259,35 @@
     core = strip % 2
     y = (strip // 2) % 2
     z = strip // 4
-    me = (x * 2 + y) * 2 + core
-
-    offsets = ((1, 1, 0), (1, 1, 1), (1, 0, 0), (1, 0, 1), (0, 1, 0), (0, 1, 1), (0, 0, 1))
-
-    def place(n):
+
+    offsets = ((1, 1, 0), (1, 1, 1), (1, 0, 0), (0, 1, 0), (1, 0, 1), (0, 1, 1), (0, 0, 1))
+
+    def plane(n):
         dx, dy, dc = offsets[n]
-        return ((x + dx) % 2, (y + dy) % 2, (core + dc) % 2)
-
-    def plane(n):
-        px, py, pc = place(n)
-        return (px, (z * 2 + py) * 2 + pc)
-
-    def slot(n):
-        px, py, pc = place(n)
-        return (px * 2 + py) * 2 + pc
+        return ((x + dx) % 2, (z * 2 + (y + dy) % 2) * 2 + (core + dc) % 2)
+
+    def block_of(dx, dy, dc):
+        return ((x + dx) % 2 * 2 + (y + dy) % 2) * 2 + (core + dc + turn(z)) % 2
+
+    def turn(zpos):
+        return ((zpos == 1) | (zpos == 2)).astype(jnp.int32)
+
+    me = block_of(0, 0, 0)
 
     def depth_dev(zpos):
         return (x, (zpos * 2 + y) * 2 + core)
 
-    x_dev = (1 - x, strip)
-    y_dev = (x, (z * 2 + 1 - y) * 2 + core)
+    def depth_swap(zpos):
+        return (x, (zpos * 2 + y) * 2 + 1 - core)
+
+    x_dev = (1 - x, (z * 2 + y) * 2 + 1 - core)
+    y_dev = (x, (z * 2 + 1 - y) * 2 + 1 - core)
     core_dev = (x, (z * 2 + y) * 2 + 1 - core)
     low_end = z == 0
     high_end = z == depth - 1
     outer = low_end | high_end
-    corner = (y == 0) & (core == 0)
+    corner_from = (y == 0) & (core == 1)
+    corner_to = (y == 0) & (core == 0)
 
     barrier = pltpu.get_barrier_semaphore()
     for device in (x_dev, y_dev, core_dev):
@@ -295,14 +295,16 @@
 
     @pl.when(jnp.logical_not(low_end))
     def _():
-        pl.semaphore_signal(barrier, inc=1, device_id=depth_dev(z - 1), device_id_type=MESH)
+        pl.semaphore_signal(barrier, inc=1, device_id=depth_swap(z - 1), device_id_type=MESH)
 
     @pl.when(jnp.logical_not(high_end))
     def _():
-        pl.semaphore_signal(barrier, inc=1, device_id=depth_dev(z + 1), device_id_type=MESH)
+        pl.semaphore_signal(barrier, inc=1, device_id=depth_swap(z + 1), device_id_type=MESH)
 
     spot = y * 2 + core
     other = (1 - y) * 2 + core
+    spot_in = y * 2 + 1 - core
+    other_in = (1 - y) * 2 + 1 - core
     loads[0].wait()
     for li in range(layer_dev):
         scr_all[x * layer_dev + li, spot] = scr_ref[li].astype(jnp.float32)
@@ -345,10 +347,6 @@
 
     to_core(scr_all.at[x * layer_dev, spot])
     to_core(scr_all.at[x * layer_dev + 1, spot])
-
-    @pl.when((z == 1) & corner)
-    def _():
-        pl.semaphore_signal(credit, inc=1, device_id=depth_dev(z - 1), device_id_type=MESH)
 
     for load in loads[1:]:
         load.wait()
@@ -397,7 +395,8 @@
         row_base = row_sub // 8 * PIXELS + row_sub % PIXELS
         row_frame = row_sub // PIXELS % FRAMES
         for zpos in range(depth):
-            pupil_row = (row_base + ((zpos * 2 + y) * 2 + core) * (arcs * PIXELS)).astype(jnp.float32)
+            held = jnp.where(z == zpos, core, 1 - core)
+            pupil_row = (row_base + ((zpos * 2 + y) * 2 + held) * (arcs * PIXELS)).astype(jnp.float32)
             for i, n in enumerate(members):
                 reach = pupil_row * shrinks[n]
                 for f in range(FRAMES):
@@ -434,16 +433,22 @@
         passed[which, h] = remote(here, here, pass_send.at[n], pass_recv.at[n], device)
 
     for h in range(HALVES):
-        here = piece((1 - x) * layer_dev, spot, h)
+        here = piece((1 - x) * layer_dev, spot_in, h)
         x_copies[0, h].wait_recv()
         pass_on(0, h, here, y_dev)
         to_core(here)
-        here = piece(x * layer_dev + 1, other, h)
+        here = piece(x * layer_dev + 1, other_in, h)
         y_copies[1, h].wait_recv()
         pass_on(1, h, here, x_dev)
         to_core(here)
     for copy in core_copies[:2]:
         copy.wait()
+
+    @pl.when(jnp.logical_not(outer))
+    def _():
+        for zpos in (z - 1, z + 1):
+            pl.semaphore_signal(credit.at[0], inc=1, device_id=depth_dev(zpos), device_id_type=MESH)
+
     for n in mine:
         across(0, n)
     acc[...] = project(0)
@@ -455,11 +460,17 @@
     for n in range(8):
         some = min(block, actuators - n * block)
         sat[n, 0, :some] = sat_raw[n * block : n * block + some]
+    pl.semaphore_wait(credit.at[0], 1)
+
+    @pl.when((z == 1) & corner_from)
+    def _():
+        pl.semaphore_signal(credit.at[1], inc=1, device_id=depth_dev(z - 1), device_id_type=MESH)
+
     for h in range(HALVES):
         x_copies[1, h].wait_recv()
-        to_core(piece((1 - x) * layer_dev + 1, spot, h))
+        to_core(piece((1 - x) * layer_dev + 1, spot_in, h))
         y_copies[0, h].wait_recv()
-        to_core(piece(x * layer_dev, other, h))
+        to_core(piece(x * layer_dev, other_in, h))
     for copy in core_copies[2 : 2 + 2 * HALVES]:
         copy.wait()
     across(1, layer_dev)
@@ -482,9 +493,6 @@
     for n in theirs:
         across(4, n)
     acc[...] += project(4)
-    for copy in list(x_copies.values()) + list(y_copies.values()) + list(passed.values()):
-        copy.wait_send()
-
     def pack(zpos):
         value = acc[pl.ds(pl.multiple_of(zpos * chunk_rows, chunk_rows), chunk_rows), :]
         for a in range(arcs):
@@ -503,39 +511,15 @@
     tiles = packed_tiles(arcs)
     pieces = [pl.ds(edge * 8, (tiles - edge) * 8), pl.ds(0, edge * 8)]
     count = len(pieces)
-    below = z < depth // 2
-    ahead = jnp.where(below, 1, -1)
-    side = jnp.where(below, 0, 1)
-    pack(z + 2 * ahead)
-    first_copies = []
-    for i, rows in enumerate(pieces):
-        first_copies.append(
-            remote(
-                part.at[z + 2 * ahead, rows],
-                relay_in.at[side, rows],
-                ra_send.at[i],
-                ra_recv.at[side * count + i],
-                depth_dev(z + ahead),
-            )
-        )
-
-    def relay_wait(s, i):
-        pltpu.make_async_remote_copy(
-            src_ref=part.at[0, pieces[i]],
-            dst_ref=relay_in.at[s, pieces[i]],
-            send_sem=ra_send.at[i],
-            recv_sem=ra_recv.at[s * count + i],
-            device_id=depth_dev(z),
-            device_id_type=MESH,
-        ).wait_recv()
-
-    def main_copy(s, i, zpos):
+    ahead = jnp.where(z < depth // 2, 1, -1)
+
+    def z_copy(send, slot_at, i, zpos):
         return pltpu.make_async_remote_copy(
             src_ref=part.at[zpos, pieces[i]],
-            dst_ref=main_in.at[s, pieces[i]],
-            send_sem=m_send.at[s * count + i],
-            recv_sem=m_recv.at[s * count + i],
-            device_id=depth_dev(zpos),
+            dst_ref=z_in.at[slot_at, pieces[i]],
+            send_sem=z_send.at[send * count + i],
+            recv_sem=z_recv.at[slot_at * count + i],
+            device_id=depth_swap(zpos),
             device_id_type=MESH,
         )
 
@@ -544,61 +528,43 @@
         dst_ref=far_in,
         send_sem=far_send,
         recv_sem=far_recv,
-        device_id=depth_dev(2),
+        device_id=depth_swap(depth - 1),
         device_id_type=MESH,
     )
-
-    @pl.when(outer)
-    def _():
-        pack(z + ahead)
-        copies = []
+    sends = [(z + 2 * ahead, 0), (z + ahead, jnp.where(outer, 2, 1))]
+    for n, (zpos, slot_at) in enumerate(sends):
+        pack(zpos)
         for i in range(count):
-            copies.append(main_copy(side, i, z + ahead))
-            copies[-1].start()
-
-        @pl.when(low_end & corner)
+            z_copy(n, slot_at, i, zpos).start()
+
+    @pl.when(jnp.logical_not(outer))
+    def _():
+        pack(z - ahead)
+        for i in range(count):
+            z_copy(2, 1, i, z - ahead).start()
+
+    @pl.when(low_end & corner_from)
+    def _():
+        pack(depth - 1)
+        pl.semaphore_wait(credit.at[1], 1)
+        far_copy.start()
+
+    pack(z)
+    for i, rows in enumerate(pieces):
+
+        @pl.when(jnp.logical_not(outer))
         def _():
-            pack(depth - 1)
-            pl.semaphore_wait(credit, 1)
-            far_copy.start()
-            far_copy.wait_send()
-
-        pack(z)
-        for i, rows in enumerate(pieces):
-            main_copy(1 - side, i, z + ahead).wait_recv()
-            phase_sc[rows] = part[z, rows] + main_in[1 - side, rows]
-        for copy in copies:
-            copy.wait_send()
-
-    @pl.when(jnp.logical_not(outer))
-    def _():
-        pack(z + 1)
-        pack(z - 1)
-        copies = []
-        for i, rows in enumerate(pieces):
-            for s in range(2):
-                to = z + 1 - 2 * s
-                relay_wait(s, i)
-                if i == 1 and s == 0:
-
-                    @pl.when((z == 2) & corner)
-                    def _():
-                        far_copy.wait_recv()
-                        part[depth - 1, rows] = part[depth - 1, rows] + far_in[...]
-
-                part[to, rows] = part[to, rows] + relay_in[s, rows]
-                copies.append(main_copy(s, i, to))
-                copies[-1].start()
-        pack(z)
-        for i, rows in enumerate(pieces):
-            for s in range(2):
-                main_copy(s, i, z + 1 - 2 * s).wait_recv()
-            phase_sc[rows] = part[z, rows] + main_in[0, rows] + main_in[1, rows]
-        for copy in copies:
-            copy.wait_send()
-
-    for copy in first_copies:
-        copy.wait_send()
+            z_copy(0, 2, i, z - ahead).wait_recv()
+            part[z, rows] = part[z, rows] + z_in[2, rows]
+
+        z_copy(0, 1, i, z + ahead).wait_recv()
+        z_copy(0, 0, i, z + 2 * ahead).wait_recv()
+        phase_sc[rows] = part[z, rows] + z_in[0, rows] + z_in[1, rows]
+
+    @pl.when(high_end & corner_to)
+    def _():
+        far_copy.wait_recv()
+        phase_sc[pieces[1]] = phase_sc[pieces[1]] + far_in[...]
 
     for a in range(arcs):
         for q in range(PIXELS):
@@ -649,32 +615,35 @@
 
     rec_copy.wait()
     rounded = [slope_sc[c].astype(jnp.bfloat16) for c in range(2)]
-    tail = actuators - 6 * block
-
-    def update(chip):
-        def some(cols, width):
+    tail = actuators - 7 * block
+    whole = tail // 128 * 128
+
+    def update(to):
+        def some(cols):
             value = jnp.dot(rounded[0], rec[0, :, cols], preferred_element_type=jnp.float32)
-            value = value + jnp.dot(rounded[1], rec[1, :, cols], preferred_element_type=jnp.float32)
-            upd[2 * chip] = value[:, :block]
-            upd[2 * chip + 1, :, : width - block] = value[:, block:]
-
-        @pl.when(chip < 3)
+            return value + jnp.dot(rounded[1], rec[1, :, cols], preferred_element_type=jnp.float32)
+
+        @pl.when(to < 7)
         def _():
-            some(pl.ds(pl.multiple_of(chip * 2 * block, 128), 2 * block), 2 * block)
-
-        @pl.when(chip == 3)
+            upd[to] = some(pl.ds(pl.multiple_of(to * block, 128), block))
+
+        @pl.when(to == 7)
         def _():
-            upd[7] = jnp.zeros_like(upd[7])
-            some(slice(6 * block, actuators), tail)
+            upd[7, :, whole:] = jnp.zeros((FRAMES, block - whole), jnp.float32)
+            upd[7, :, :tail] = some(slice(7 * block, actuators))
+
+    def b_dev(zpos):
+        return (x, (zpos * 2 + y) * 2 + (core + turn(z) + turn(zpos)) % 2)
 
     copies = []
     for n in range(7):
-        to = slot(n)
-        if n % 2 == 0:
-            update(to // 2)
+        to = block_of(*offsets[n])
+        update(to)
         copies.append(remote(upd.at[to], gathered.at[n], a_send.at[n], a_recv.at[n], plane(n)))
+    update(me)
     for copy in copies:
-        copy.wait()
+        copy.wait_recv()
+    drain = copies
     total = upd[me]
     for n in range(7):
         total = total + gathered[n]
@@ -682,10 +651,11 @@
     copies = []
     for k in range(1, depth):
         copies.append(
-            remote(zsum.at[z], zsum.at[z], b_send.at[k - 1], b_recv.at[k - 1], depth_dev((z + k) % depth))
+            remote(zsum.at[z], zsum.at[z], b_send.at[k - 1], b_recv.at[k - 1], b_dev((z + k) % depth))
         )
     for copy in copies:
-        copy.wait()
+        copy.wait_recv()
+    drain = drain + copies
     total = zsum[0]
     for k in range(1, depth):
         total = total + zsum[k]
@@ -701,8 +671,25 @@
         copies.append(
             remote(upd_out.at[:, own_cols], upd_out.at[:, own_cols], c_send.at[n], c_recv.at[n], plane(n))
         )
+    for copy in list(x_copies.values()) + list(y_copies.values()) + list(passed.values()):
+        copy.wait_send()
+    for n, (zpos, slot_at) in enumerate(sends):
+        for i in range(count):
+            z_copy(n, slot_at, i, zpos).wait_send()
+
+    @pl.when(jnp.logical_not(outer))
+    def _():
+        for i in range(count):
+            z_copy(2, 1, i, z - ahead).wait_send()
+
+    @pl.when(low_end & corner_from)
+    def _():
+        far_copy.wait_send()
+
     for copy in copies:
         copy.wait()
+    for copy in drain:
+        copy.wait_send()
 
 
 def fused_shards(screens, row_offset, col_offset, layer_bin, illumination, reconstructor, sat_code):
@@ -744,8 +731,7 @@
             pltpu.VMEM((contraction, PUPIL_PIX), jnp.bfloat16),
             pltpu.VMEM((depth * rows, PUPIL_PIX), jnp.float32),
             pltpu.VMEM((depth,) + chunk, jnp.float32),
-            pltpu.VMEM((2,) + chunk, jnp.float32),
-            pltpu.VMEM((2,) + chunk, jnp.float32),
+            pltpu.VMEM((3,) + chunk, jnp.float32),
             pltpu.VMEM(edge, jnp.float32),
             pltpu.VMEM(chunk, jnp.float32),
             pltpu.VMEM((PIXELS, FRAMES * PIXELS, count_here), jnp.float32),
@@ -761,8 +747,8 @@
             dma((2 * layer_dev * HALVES,)), dma((2 * layer_dev * HALVES,)),
             dma((2 * HALVES,)), dma((2 * HALVES,)),
             dma((2 + 6 * HALVES,)), dma((2 + 6 * HALVES,)),
-            dma((2,)), dma((4,)), dma((4,)), dma((4,)), dma, dma,
-            pltpu.SemaphoreType.REGULAR,
+            dma((6,)), dma((6,)), dma, dma,
+            pltpu.SemaphoreType.REGULAR((2,)),
             dma((7,)), dma((7,)),
             dma((depth - 1,)), dma((depth - 1,)),
             dma((7,)), dma((7,)),

time: 34 us -> 31.4 us (0.924)
  Pallas kernels: 32 us -> 29.4 us
    pallas_call x1, Pallas kernels: 32 us -> 29.4 us  [fused_shards(): pl.pallas_call(functools.partial(fused_kernel, block), out_shape=(jax.Sha...]
where the time goes in v3:
time: 31.4 us; the launch traced here: 31.3 us
  Pallas kernels  29.4 us (94%)
  local copies, waits for them, and re-layouts  1.22 us (4%)
  between operations  0.64 us (2%)
    pallas_call x1, Pallas kernels, fused_shards(): pl.pallas_call(functools.partial(fused_kernel, block), out_shape=(jax.Sha...  29.4 us

profile of v3, /device:TPU:0, one launch (start us, length us, event | category | flops | bytes accessed | tf_op | source)
XLA Modules:
  0.0 31.3 jit_solution(16076133489714628832)
XLA Ops:
  0.6 29.4 %fused.1 = (f32[2,2,400]{2,1,0:T(2,128)S(1)}, f32[2,6144]{1,0:T(2,128)S(1)}) custom-call(bf16[2,32,512]{2,1,0:T(8,128)(2,1)} %scr_hbm.1, s32[2,2,4]{2,1,0:T(2,128)} %bitcast.2, s32[2,2,4]{2,1,0:T(2,128)} %bitcast.3, s32[4]{0:T(128)} %bin_hbm.1, f32[16,400]{1,0:T(8,128)} %ill_hbm.1, bf16[2,400,6000]{2,1,0:T(8,128)(2,1)} %rec_hbm.1, s32[6000]{0:T(1024)} %sat_hbm.1), custom_call_target="tpu_custom_call" | custom-call | tf_op jit(solution)/shard_map/fused/pallas_call | solution.py:714
  30.0 0.6 %slice.3 = f32[2,6000]{1,0:T(2,128)} slice(f32[2,6144]{1,0:T(2,128)S(1)} %get-tuple-element.5), slice={[0:2], [0:6000]} | slice | bytes 96000 | tf_op jit(solution)/shard_map/slice | solution.py:767
  30.7 0.6 %copy.10 = f32[2,2,400]{2,1,0:T(2,128)} copy(f32[2,2,400]{2,1,0:T(2,128)S(1)} %get-tuple-element.8) | data formatting | bytes 12800

commit v4 on v3

--- a/solution.py
+++ b/solution.py
@@ -532,16 +532,19 @@
         device_id_type=MESH,
     )
     sends = [(z + 2 * ahead, 0), (z + ahead, jnp.where(outer, 2, 1))]
-    for n, (zpos, slot_at) in enumerate(sends):
-        pack(zpos)
-        for i in range(count):
-            z_copy(n, slot_at, i, zpos).start()
-
     @pl.when(jnp.logical_not(outer))
     def _():
         pack(z - ahead)
         for i in range(count):
             z_copy(2, 1, i, z - ahead).start()
+
+    pack(sends[0][0])
+    for i in range(count):
+        z_copy(0, sends[0][1], i, sends[0][0]).start()
+
+    pack(sends[1][0])
+    for i in range(count):
+        z_copy(1, sends[1][1], i, sends[1][0]).start()
 
     @pl.when(low_end & corner_from)
     def _():

time: 31.4 us -> 31.3 us (level)
  no operation moved by 1% of the time
where the time goes in v4:
time: 31.3 us; the launch traced here: 31.2 us
  Pallas kernels  29.3 us (94%)
  local copies, waits for them, and re-layouts  1.22 us (4%)
  between operations  0.64 us (2%)
    pallas_call x1, Pallas kernels, fused_shards(): pl.pallas_call(functools.partial(fused_kernel, block), out_shape=(jax.Sha...  29.3 us

profile of v4, /device:TPU:0, one launch (start us, length us, event | category | flops | bytes accessed | tf_op | source)
XLA Modules:
  0.0 31.2 jit_solution(15574526271847464930)
XLA Ops:
  0.6 29.3 %fused.1 = (f32[2,2,400]{2,1,0:T(2,128)S(1)}, f32[2,6144]{1,0:T(2,128)S(1)}) custom-call(bf16[2,32,512]{2,1,0:T(8,128)(2,1)} %scr_hbm.1, s32[2,2,4]{2,1,0:T(2,128)} %bitcast.2, s32[2,2,4]{2,1,0:T(2,128)} %bitcast.3, s32[4]{0:T(128)} %bin_hbm.1, f32[16,400]{1,0:T(8,128)} %ill_hbm.1, bf16[2,400,6000]{2,1,0:T(8,128)(2,1)} %rec_hbm.1, s32[6000]{0:T(1024)} %sat_hbm.1), custom_call_target="tpu_custom_call" | custom-call | tf_op jit(solution)/shard_map/fused/pallas_call | solution.py:717
  30.0 0.6 %slice.3 = f32[2,6000]{1,0:T(2,128)} slice(f32[2,6144]{1,0:T(2,128)S(1)} %get-tuple-element.5), slice={[0:2], [0:6000]} | slice | bytes 96000 | tf_op jit(solution)/shard_map/slice | solution.py:770
  30.6 0.6 %copy.10 = f32[2,2,400]{2,1,0:T(2,128)} copy(f32[2,2,400]{2,1,0:T(2,128)S(1)} %get-tuple-element.8) | data formatting | bytes 12800

commit v5 on v4

--- a/solution.py
+++ b/solution.py
@@ -270,7 +270,7 @@
         return ((x + dx) % 2 * 2 + (y + dy) % 2) * 2 + (core + dc + turn(z)) % 2
 
     def turn(zpos):
-        return ((zpos == 1) | (zpos == 2)).astype(jnp.int32)
+        return (zpos >= depth // 2).astype(jnp.int32)
 
     me = block_of(0, 0, 0)
 

time: 31.3 us -> 31.2 us (level)
  no operation moved by 1% of the time
where the time goes in v5:
time: 31.2 us; the launch traced here: 31 us
  Pallas kernels  29.2 us (94%)
  local copies, waits for them, and re-layouts  1.22 us (4%)
  between operations  0.64 us (2%)
    pallas_call x1, Pallas kernels, fused_shards(): pl.pallas_call(functools.partial(fused_kernel, block), out_shape=(jax.Sha...  29.2 us
    slice x1, local copies, waits for them, and re-layouts, fused_shards(): return (slopes, updates[:, :actuators])  0.62 us

profile of v5, /device:TPU:0, one launch (start us, length us, event | category | flops | bytes accessed | tf_op | source)
XLA Modules:
  0.0 31.0 jit_solution(9012624424623647368)
XLA Ops:
  0.6 29.2 %fused.1 = (f32[2,2,400]{2,1,0:T(2,128)S(1)}, f32[2,6144]{1,0:T(2,128)S(1)}) custom-call(bf16[2,32,512]{2,1,0:T(8,128)(2,1)} %scr_hbm.1, s32[2,2,4]{2,1,0:T(2,128)} %bitcast.2, s32[2,2,4]{2,1,0:T(2,128)} %bitcast.3, s32[4]{0:T(128)} %bin_hbm.1, f32[16,400]{1,0:T(8,128)} %ill_hbm.1, bf16[2,400,6000]{2,1,0:T(8,128)(2,1)} %rec_hbm.1, s32[6000]{0:T(1024)} %sat_hbm.1), custom_call_target="tpu_custom_call" | custom-call | tf_op jit(solution)/shard_map/fused/pallas_call | solution.py:717
  29.8 0.6 %slice.3 = f32[2,6000]{1,0:T(2,128)} slice(f32[2,6144]{1,0:T(2,128)S(1)} %get-tuple-element.5), slice={[0:2], [0:6000]} | slice | bytes 96000 | tf_op jit(solution)/shard_map/slice | solution.py:770
  30.4 0.6 %copy.10 = f32[2,2,400]{2,1,0:T(2,128)} copy(f32[2,2,400]{2,1,0:T(2,128)S(1)} %get-tuple-element.8) | data formatting | bytes 12800
